TPU v7x, 32 devices: a whole 2x2x4 slice. The times are simulated.
32 devices in a mesh: group: 2 (over y), sta: 4 (over z), win: 2 (over x), freq: 2 (over core).
Axes of the slice: x: 2, y: 2, z: 4, core: 2. Of those that a mesh axis runs over, the one named last changes fastest.
Arguments:
- records: float32 [1024, 4, 3600], P(('group', 'sta'), 'win', 'freq'), parts along dimension 0, may hold values from -6 to 6
- valid_counts: int32 [8], P(('group', 'sta')), parts along dimension 0, may hold values from 64 to 128, as said below
- pair_blocks: int32 [8, 2], P('group'), parts along dimension 0, may hold values from 0 to 3, as said below
Outputs:
- pair_spectra: bfloat16 [8, 2, 256, 2, 128, 128], P(('group', 'sta'), 'freq', 'win'), parts along dimension 0
There are 2 independent parts, one for each index of `group`. A program takes and returns all parts, laid end to end along the dimension named above; each array names one. Nothing has to cross between parts.
Inputs may be any that keep to these rules, and one draw needn't show every extreme that they name: The stations of block i at positions below valid_counts[i] are live, the others are masked out. `pair_blocks`: slot k belongs to index k // 1 of sta and names two station blocks.
All inputs are finite; a program needn't handle non-finite values.
Results may differ from a plain program's by a relative error of at most 0.001.
Values may be sent and summed in bfloat16 or wider, within the bound.
A program may use at most 64 MiB of HBM per device.

v0:
```python
import math
import jax
import jax.numpy as jnp
from jax import lax
from jax.sharding import PartitionSpec as P

SAMPLES = 3600
BINS = 512
HALF_WIDTH = 10
TWO_PI = 2.0 * math.pi
AMP_FLOOR = 0.1
PRECISE = lax.Precision.HIGHEST


def padded_2(value, sides, width):
    for axis, dim in sides:
        peers, length = (lax.axis_size(axis), value.shape[dim])
        up = [(i, (i + 1) % peers) for i in range(peers - 1)]
        down = [(j, i) for i, j in up]
        last = lax.slice_in_dim(value, length - width, length, axis=dim)
        first = lax.slice_in_dim(value, 0, width, axis=dim)
        before = lax.ppermute(last, axis, up)
        after = lax.ppermute(first, axis, down)
        value = jnp.concatenate([before, value, after], axis=dim)
    return value


def taper_of(sample_index, length_all):
    edge_len = length_all // 20
    position = jnp.minimum(sample_index, length_all - 1 - sample_index)
    ramped = 0.5 * (1.0 - jnp.cos(math.pi * (position.astype(jnp.float32) + 0.5) / edge_len))
    return jnp.where(position < edge_len, ramped, 1.0)


def dft_tables(bin_start, amount, sample_count, length_all):
    bin_index = bin_start + 1 + lax.broadcasted_iota(jnp.int32, (amount, sample_count), 0)
    sample_index = lax.broadcasted_iota(jnp.int32, (amount, sample_count), 1)
    angles = (bin_index * sample_index % length_all).astype(jnp.float32) * (TWO_PI / length_all)
    weight = taper_of(sample_index, length_all) / math.sqrt(length_all)
    return (jnp.cos(angles) * weight, -jnp.sin(angles) * weight)


def cross_pair(left_block, right_block):
    left_real = left_block[:, :, 0]
    left_imag = left_block[:, :, 1]
    stacked = jnp.stack(
        (jnp.stack((left_real, left_imag), 2), jnp.stack((left_imag, -left_real), 2)), 1
    )
    factor = 1.0 / math.sqrt(left_block.shape[1])
    return jnp.einsum("fpwqa,fwqb->fpab", stacked, right_block, precision=PRECISE) * factor


def local(records, valid_counts, pair_blocks):
    block_size = records.shape[0]
    band_bins = BINS // lax.axis_size("freq")
    first_bin = lax.axis_index("freq") * band_bins
    portion = lax.all_gather(records, "freq", axis=2, tiled=True)
    cos_table, sin_table = dft_tables(first_bin, band_bins, portion.shape[2], SAMPLES)
    real_part = jnp.einsum("kn,swn->kws", cos_table, portion, precision=PRECISE)
    imag_part = jnp.einsum("kn,swn->kws", sin_table, portion, precision=PRECISE)
    spectrum = jnp.stack((real_part, imag_part), 2)
    live_mask = (lax.broadcasted_iota(jnp.int32, (block_size,), 0) < valid_counts[0]).astype(
        jnp.float32
    )
    spectrum = spectrum * live_mask
    magnitude = jnp.sqrt(
        spectrum[:, :, 0] * spectrum[:, :, 0] + spectrum[:, :, 1] * spectrum[:, :, 1]
    )
    padded = padded_2(magnitude, (("freq", 0),), HALF_WIDTH)
    row_index = lax.broadcasted_iota(jnp.int32, (band_bins, band_bins + 2 * HALF_WIDTH), 0)
    col_index = lax.broadcasted_iota(jnp.int32, (band_bins, band_bins + 2 * HALF_WIDTH), 1)
    box_matrix = ((col_index - row_index >= 0) & (col_index - row_index <= 2 * HALF_WIDTH)).astype(
        jnp.float32
    )
    summed = jnp.einsum("ij,jws->iws", box_matrix, padded, precision=PRECISE)
    global_bin = first_bin + lax.broadcasted_iota(jnp.int32, (band_bins,), 0)
    counted = (
        jnp.minimum(global_bin + HALF_WIDTH, BINS - 1) - jnp.maximum(global_bin - HALF_WIDTH, 0) + 1
    ).astype(jnp.float32)
    smooth = summed / counted[:, None, None]
    whitened = spectrum / jnp.maximum(smooth, AMP_FLOOR)[:, :, None, :]
    sta_count = lax.axis_size("sta")
    slots = pair_blocks.shape[0] // sta_count
    my_slots = lax.dynamic_slice_in_dim(pair_blocks, lax.axis_index("sta") * slots, slots, 0)
    held_block = lax.all_to_all(whitened, "win", split_axis=0, concat_axis=1, tiled=True)
    blank_pair = jnp.zeros((slots,) + held_block.shape, jnp.float32)
    carried = (blank_pair, blank_pair)
    portion = lax.all_gather(held_block[None], "sta", axis=0, tiled=True)
    amount = portion.shape[0]
    chosen = []
    for column in range(2):
        wanted = my_slots[:, column]
        inside = (wanted >= 0) & (wanted < amount)
        fetched = jnp.take(portion, jnp.clip(wanted, 0, amount - 1), axis=0)
        chosen.append(jnp.where(inside[:, None, None, None, None], fetched, carried[column]))
    left_blocks = chosen[0]
    right_blocks = chosen[1]
    mixed = jax.vmap(cross_pair)(left_blocks, right_blocks).astype(jnp.bfloat16)
    return mixed[:, None]


def solution(mesh):
    in_specs = (P(("group", "sta"), "win", "freq"), P(("group", "sta")), P("group", None))
    out_specs = P(("group", "sta"), "freq", "win", None, None, None)
    return jax.shard_map(local, mesh=mesh, in_specs=in_specs, out_specs=out_specs, check_vma=False)
```

profile of v0, /device:TPU:0, one launch (start us, length us, event | category | flops | bytes accessed | tf_op | source)
XLA Modules:
  0.0 175.7 jit_solution(15182454830260234039)
XLA Ops:
  6.5 0.7 all-gather.3.cloned.1.call-update
  8.0 0.1 subtract_multiply_fusion
  8.1 16.5 %all-gather.3.cloned.1.call-done = f32[128,2,3600]{0,2,1:T(8,128)} async-done(((f32[128,2,1800]{0,2,1:T(8,128)}), f32[128,2,3600]{0,2,1:T(8,128)}) %all-gather.3.cloned.1.call-update) | async-done | bytes 3686416 | tf_op jit(solution)/shard_map/all_gather | solution.py:57
  24.6 25.0 %fusion.37 = f32[256,2,1,128]{3,0,1,2:T(8,128)S(1)} fusion(f32[128,2,3600]{0,2,1:T(8,128)} %all-gather.3.cloned.1.call-done, f32[3600]{0:T(1024)S(1)} %subtract_multiply_fusion, s32[256]{0:T(256)S(1)} %iota_add_fusion, pred[3600]{0:T(1024)(128)(4,1)S(1)} %fusion.65), kind=kOutput, calls=%fused_computation.35 | convolution fusion | flops 2843136000 | bytes 3967568 | tf_op jit(solution)/shard_map/kn,swn->kws/dot_general | solution.py:60
  49.6 21.3 %fusion.34 = f32[256,2,1,128]{3,0,1,2:T(8,128)S(1)} fusion(f32[128,2,3600]{0,2,1:T(8,128)S(1)} %copy-done.1, f32[3600]{0:T(1024)S(1)} %subtract_multiply_fusion, s32[256]{0:T(256)S(1)} %iota_add_fusion, pred[3600]{0:T(1024)(128)(4,1)S(1)} %fusion.65), kind=kOutput, calls=%fused_computation.34 | convolution fusion | flops 2842214400 | bytes 3967568 | tf_op jit(solution)/shard_map/kn,swn->kws/dot_general | solution.py:59
  70.9 0.1 fusion.58
  71.1 2.1 %collective-permute-start = (f32[10,2,128]{2,0,1:T(8,128)S(1)}, f32[10,2,128]{2,0,1:T(8,128)S(1)}, u32[]{:S(2)}, u32[]{:S(2)}) collective-permute-start(f32[10,2,128]{2,0,1:T(8,128)S(1)} %get-tuple-element.21), channel_id=1, source_target_pairs={{0,1},{2,3},{4,5},{6,7},{8,9},{10,11},{12,13},{14,15},{16,17},{18,... | collective-permute-start | bytes 30728 | tf_op jit(solution)/shard_map/ppermute | solution.py:22
  73.2 1.3 collective-permute-start.1
  74.5 0.1 fusion.86
  74.6 1.7 collective-permute-done.1
  76.3 0.5 fusion.40
  76.8 0.1 broadcast_divide_fusion
  76.8 0.4 copy.6
  77.3 11.3 %all_to_all.15 = f32[256,2,2,128]{3,1,2,0:T(2,128)S(1)} all-to-all(f32[256,2,2,128]{3,1,2,0:T(2,128)S(1)} %copy.6), channel_id=1, replica_groups=mesh['group'=2,'sta'=4,'win'=2,'freq'=2] {'win'}, dimensions={0} | all-to-all | bytes 1048576 | tf_op jit(solution)/shard_map/all_to_all | solution.py:85
  88.5 0.8 copy.7
  89.4 0.1 constant_dynamic-slice_fusion.2
  89.4 0.5 fusion.82
  93.5 42.0 %all-gather.5.cloned.1.call-done = f32[4,128,4,2,128]{4,1,3,2,0:T(8,128)} async-done(((f32[1,128,4,2,128]{4,1,3,2,0:T(8,128)}), f32[4,128,4,2,128]{4,1,3,2,0:T(8,128)}) %all-gather.5.cloned.1.call-update) | async-done | bytes 2097168 | tf_op jit(solution)/shard_map/all_gather | solution.py:88
  135.6 1.3 constant_dynamic-slice_fusion
  136.8 0.5 fusion.85
  137.3 0.5 fusion.45
  137.8 0.1 fusion.81
  137.9 0.1 maximum_bitcast_fusion.1
  138.0 30.8 %fusion.1 = bf16[1,1,128,2,128,128]{5,4,3,2,1,0:T(8,128)(2,1)} fusion(f32[1,128,4,2,128]{4,1,3,2,0:T(8,128)S(1)} %get-tuple-element.17, pred[]{:T(512)} %bitcast.23, pred[]{:T(512)} %bitcast.21, f32[1,128,1,4,2,128]{5,3,4,1,2,0:T(4,128)S(1)} %maximum_bitcast_fusion.1, f32[1,128,1,4,2,128]{5,3,4,1,2,0:T(4,128)S(1)} %fusion.85), kind=kOutput, calls=%fused_computation.3 | convolution fusion | flops 411566080 | bytes 9961474 | tf_op jit(solution)/shard_map/vmap(fpwqa,fwqb->fpab)/dot_general | solution.py:50
  (14 shorter events, 0.1 us)
Async XLA Ops:
  6.5 82.8 %copy-start = (s32[4,2]{0,1:T(2,128)S(1)}, s32[4,2]{0,1:T(2,128)}, u32[]{:S(2)}) copy-start(s32[4,2]{0,1:T(2,128)} %param.7) | copy-start | bytes 100
  6.5 18.0 %all-gather.3.cloned.1.call-start = ((), (), s32[]{:S(2)}) async-start(), calls=%async_computation.1 | async-start | bytes 5529600 | tf_op jit(solution)/shard_map/all_gather | solution.py:57
  7.3 128.3 %all-gather.5.cloned.1.call-start = ((), (), s32[]{:S(2)}) async-start(), calls=%async_computation.2 | async-start | bytes 2621440 | tf_op jit(solution)/shard_map/all_gather | solution.py:88
  24.6 25.0 %copy-start.1 = (f32[128,2,3600]{0,2,1:T(8,128)S(1)}, f32[128,2,3600]{0,2,1:T(8,128)}, u32[]{:S(2)}) copy-start(f32[128,2,3600]{0,2,1:T(8,128)} %all-gather.3.cloned.1.call-done) | copy-start | bytes 11059204
  71.1 3.5 %collective-permute-start = (f32[10,2,128]{2,0,1:T(8,128)S(1)}, f32[10,2,128]{2,0,1:T(8,128)S(1)}, u32[]{:S(2)}, u32[]{:S(2)}) collective-permute-start(f32[10,2,128]{2,0,1:T(8,128)S(1)} %get-tuple-element.21), channel_id=1, source_target_pairs={{0,1},{2,3},{4,5},{6,7},{8,9},{10,11},{12,13},{14,15},{16,17},{18,... | collective-permute-start | bytes 30728 | tf_op jit(solution)/shard_map/ppermute | solution.py:22
  73.2 3.1 %collective-permute-start.1 = (f32[10,2,128]{2,0,1:T(8,128)S(1)}, f32[10,2,128]{2,0,1:T(8,128)S(1)}, u32[]{:S(2)}, u32[]{:S(2)}) collective-permute-start(f32[10,2,128]{2,0,1:T(8,128)S(1)} %get-tuple-element.22), channel_id=1, source_target_pairs={{1,0},{3,2},{5,4},{7,6},{9,8},{11,10},{13,12},{15,14},{17,16},{19,... | collective-permute-start | bytes 30728 | tf_op jit(solution)/shard_map/ppermute | solution.py:23
Sparse Core Ops, SparseCore 0:
  8.9 15.6 all-gather.2
  89.5 46.0 all-gather.4
where the time goes:
time: 176 us
  matrix products  77.6 us (44%)
  waiting for transfers between devices  60.9 us (35%)
  between operations  17.8 us (10%)
  blocking collectives  11.3 us (6%)
  starting transfers between devices  3.45 us (2%)
  local copies, waits for them, and re-layouts  3.12 us (2%)
    all_gather x1, waiting for transfers between devices, local(): portion = lax.all_gather(held_block[None], 'sta', axis=0, tiled=True)  42 us
    dot_general x1, matrix products, cross_pair(): jnp.einsum('fpwqa,fwqb->fpab', stacked, right_block, precision=PRECISE)  30.8 us
    dot_general x1, matrix products, local(): imag_part = jnp.einsum('kn,swn->kws', sin_table, portion, precision=PRECISE)  25 us
    dot_general x1, matrix products, local(): real_part = jnp.einsum('kn,swn->kws', cos_table, portion, precision=PRECISE)  21.3 us
    all_gather x1, waiting for transfers between devices, local(): portion = lax.all_gather(records, 'freq', axis=2, tiled=True)  16.5 us
    all_to_all x1, blocking collectives, local(): lax.all_to_all(whitened, 'win', split_axis=0, concat_axis=1, tiled=True)  11.3 us
  transfers between devices with their start and end apart: 4, of which 3 were waited for; matrix products, arithmetic and copies ran while one was open for 0% of the time, Pallas kernels for 0%

commit v1 on v0

--- a/solution.py
+++ b/solution.py
@@ -1,8 +1,10 @@
+import functools
 import math
 import jax
 import jax.numpy as jnp
 from jax import lax
 from jax.sharding import PartitionSpec as P
+from jax.lax import axis_index, axis_size, ppermute
 
 SAMPLES = 3600
 BINS = 512
@@ -10,6 +12,34 @@
 TWO_PI = 2.0 * math.pi
 AMP_FLOOR = 0.1
 PRECISE = lax.Precision.HIGHEST
+
+
+def recast_windows(shard_in, ax_name):
+    b_now, e_next, n_now = (axis_size(ax_name), axis_index(ax_name), shard_in.shape[0])
+    lanes = []
+    for dd in tuple(range(b_now)):
+        lanes.append((dd, (dd + 1) % b_now))
+    line_up = []
+    for dd in [*range(b_now)]:
+        line_up.append((dd, (dd - 1) % b_now))
+    value_now = jnp.zeros((*shard_in.shape[:0], b_now * n_now, *shard_in.shape[1:]), shard_in.dtype)
+    value_now = lax.dynamic_update_slice_in_dim(value_now, shard_in, e_next * n_now, axis=0)
+    frame_out = arr_out = shard_in
+    tile_out = b_now // 2
+    for k0 in tuple(range(1, tile_out + 1)):
+        frame_out = ppermute(frame_out, ax_name, lanes)
+        value_now = lax.dynamic_update_slice_in_dim(
+            value_now, frame_out, (e_next - k0) % b_now * n_now, axis=0
+        )
+        if k0 < b_now - tile_out:
+            arr_out = ppermute(arr_out, ax_name, line_up)
+            value_now = lax.dynamic_update_slice_in_dim(
+                value_now, arr_out, (e_next + k0) % b_now * n_now, axis=0
+            )
+    return value_now
+
+
+streams_draft = functools.partial(recast_windows, ax_name="sta")
 
 
 def padded_2(value, sides, width):
@@ -85,7 +115,7 @@
     held_block = lax.all_to_all(whitened, "win", split_axis=0, concat_axis=1, tiled=True)
     blank_pair = jnp.zeros((slots,) + held_block.shape, jnp.float32)
     carried = (blank_pair, blank_pair)
-    portion = lax.all_gather(held_block[None], "sta", axis=0, tiled=True)
+    portion = streams_draft(held_block[None])
     amount = portion.shape[0]
     chosen = []
     for column in range(2):

time: 176 us -> 165 us (0.938)
  waiting for transfers between devices: 60.9 us -> 47.3 us
  starting transfers between devices: 3.45 us -> 7.29 us
    all_gather x1 -> x0, waiting for transfers between devices: 42 us -> none  [local(): portion = lax.all_gather(held_block[None], 'sta', axis=0, tiled=True)]
    ppermute x0 -> x3, waiting for transfers between devices: none -> 28.4 us  [the longest x2 23 us: recast_windows(): frame_out = ppermute(frame_out, ax_name, lanes)]
    ppermute x0 -> x3, starting transfers between devices: none -> 3.88 us  [the longest x1 2.18 us: recast_windows(): arr_out = ppermute(arr_out, ax_name, line_up)]
  transfers between devices with their start and end apart: 4 -> 6, of which waited for: 3 -> 5; matrix products, arithmetic and copies ran while one was open for 0% -> 1% of each run, Pallas kernels for 0% -> 0%
where the time goes in v1:
time: 165 us; the launch traced here: 164 us
  matrix products  77.8 us (47%)
  waiting for transfers between devices  47.3 us (29%)
  between operations  18.1 us (11%)
  blocking collectives  11.2 us (7%)
  starting transfers between devices  7.29 us (4%)
  local copies, waits for them, and re-layouts  1.78 us (1%)
    dot_general x1, matrix products, cross_pair(): jnp.einsum('fpwqa,fwqb->fpab', stacked, right_block, precision=PRECISE)  31 us
    dot_general x1, matrix products, local(): imag_part = jnp.einsum('kn,swn->kws', sin_table, portion, precision=PRECISE)  25 us
    ppermute x2, waiting for transfers between devices, recast_windows(): frame_out = ppermute(frame_out, ax_name, lanes)  23 us
    dot_general x1, matrix products, local(): real_part = jnp.einsum('kn,swn->kws', cos_table, portion, precision=PRECISE)  21.3 us
    all_gather x1, waiting for transfers between devices, local(): portion = lax.all_gather(records, 'freq', axis=2, tiled=True)  16.5 us
    all_to_all x1, blocking collectives, local(): lax.all_to_all(whitened, 'win', split_axis=0, concat_axis=1, tiled=True)  11.2 us
    ppermute x1, waiting for transfers between devices, recast_windows(): arr_out = ppermute(arr_out, ax_name, line_up)  5.43 us
  transfers between devices with their start and end apart: 6, of which 5 were waited for; matrix products, arithmetic and copies ran while one was open for 1% of the time, Pallas kernels for 0%

profile of v1, /device:TPU:0, one launch (start us, length us, event | category | flops | bytes accessed | tf_op | source)
XLA Modules:
  0.0 164.4 jit_solution(17804319026015250266)
XLA Ops:
  6.5 0.7 all-gather.2.cloned.1.call-update
  8.0 16.5 %all-gather.2.cloned.1.call-done = f32[128,2,3600]{0,2,1:T(8,128)} async-done(((f32[128,2,1800]{0,2,1:T(8,128)}), f32[128,2,3600]{0,2,1:T(8,128)}) %all-gather.2.cloned.1.call-update) | async-done | bytes 3686416 | tf_op jit(solution)/shard_map/all_gather | solution.py:87
  24.6 25.0 %fusion.37 = f32[256,2,1,128]{3,0,1,2:T(8,128)S(1)} fusion(f32[128,2,3600]{0,2,1:T(8,128)} %all-gather.2.cloned.1.call-done, f32[3600]{0:T(1024)S(1)} %subtract_multiply_fusion, s32[256]{0:T(256)S(1)} %iota_add_fusion, pred[3600]{0:T(1024)(128)(4,1)S(1)} %fusion.63), kind=kOutput, calls=%fused_computation.35 | convolution fusion | flops 2843136000 | bytes 3967568 | tf_op jit(solution)/shard_map/kn,swn->kws/dot_general | solution.py:90
  49.6 21.3 %fusion.34 = f32[256,2,1,128]{3,0,1,2:T(8,128)S(1)} fusion(f32[128,2,3600]{0,2,1:T(8,128)S(1)} %copy-done.1, f32[3600]{0:T(1024)S(1)} %subtract_multiply_fusion, s32[256]{0:T(256)S(1)} %iota_add_fusion, pred[3600]{0:T(1024)(128)(4,1)S(1)} %fusion.63), kind=kOutput, calls=%fused_computation.34 | convolution fusion | flops 2842214400 | bytes 3967568 | tf_op jit(solution)/shard_map/kn,swn->kws/dot_general | solution.py:89
  71.0 0.1 fusion.56
  71.1 2.1 %collective-permute-start = (f32[10,2,128]{2,0,1:T(8,128)S(1)}, f32[10,2,128]{2,0,1:T(8,128)S(1)}, u32[]{:S(2)}, u32[]{:S(2)}) collective-permute-start(f32[10,2,128]{2,0,1:T(8,128)S(1)} %get-tuple-element.19), channel_id=1, source_target_pairs={{0,1},{2,3},{4,5},{6,7},{8,9},{10,11},{12,13},{14,15},{16,17},{18,... | collective-permute-start | bytes 30728 | tf_op jit(solution)/shard_map/ppermute | solution.py:52
  73.2 1.3 collective-permute-start.1
  74.6 1.7 %collective-permute-done.1 = f32[10,2,128]{2,0,1:T(8,128)S(1)} collective-permute-done((f32[10,2,128]{2,0,1:T(8,128)S(1)}, f32[10,2,128]{2,0,1:T(8,128)S(1)}, u32[]{:S(2)}, u32[]{:S(2)}) %collective-permute-start.1) | collective-permute-done | bytes 10272 | tf_op jit(solution)/shard_map/ppermute | solution.py:53
  76.3 0.5 fusion.40
  76.8 0.4 copy.6
  77.3 11.2 %all_to_all.15 = f32[256,2,2,128]{3,1,2,0:T(2,128)S(1)} all-to-all(f32[256,2,2,128]{3,1,2,0:T(2,128)S(1)} %copy.6), channel_id=1, replica_groups=mesh['group'=2,'sta'=4,'win'=2,'freq'=2] {'win'}, dimensions={0} | all-to-all | bytes 1048576 | tf_op jit(solution)/shard_map/all_to_all | solution.py:115
  88.4 0.2 copy.7
  88.6 1.7 %collective-permute-start.2 = (f32[1,128,4,2,128]{4,2,3,1,0:T(4,128)S(1)}, f32[1,128,4,2,128]{4,2,3,1,0:T(4,128)S(1)}, u32[]{:S(2)}, u32[]{:S(2)}) collective-permute-start(f32[1,128,4,2,128]{4,2,3,1,0:T(4,128)S(1)} %bitcast.66), channel_id=1, source_target_pairs={{0,4},{4,8},{8,12},{12,0},{1,5},{5,9},{9,13},{13,1},{2,6},{6,10},{... | collective-permute-start | bytes 1572872 | tf_op jit(solution)/shard_map/ppermute | solution.py:30
  90.3 2.2 %collective-permute-start.3 = (f32[1,128,4,2,128]{4,2,3,1,0:T(4,128)S(1)}, f32[1,128,4,2,128]{4,2,3,1,0:T(4,128)S(1)}, u32[]{:S(2)}, u32[]{:S(2)}) collective-permute-start(f32[1,128,4,2,128]{4,2,3,1,0:T(4,128)S(1)} %bitcast.67), channel_id=1, source_target_pairs={{0,12},{4,0},{8,4},{12,8},{1,13},{5,1},{9,5},{13,9},{2,14},{6,2},{... | collective-permute-start | bytes 1572872 | tf_op jit(solution)/shard_map/ppermute | solution.py:35
  92.5 12.9 %collective-permute-done.2 = f32[1,128,4,2,128]{4,2,3,1,0:T(4,128)S(1)} collective-permute-done((f32[1,128,4,2,128]{4,2,3,1,0:T(4,128)S(1)}, f32[1,128,4,2,128]{4,2,3,1,0:T(4,128)S(1)}, u32[]{:S(2)}, u32[]{:S(2)}) %collective-permute-start.2) | collective-permute-done | bytes 524320 | tf_op jit(solution)/shard_map/ppermute | solution.py:30
  105.5 0.6 fusion.81
  109.9 0.3 broadcast_in_dim.47
  110.3 5.4 %collective-permute-done.3 = f32[1,128,4,2,128]{4,2,3,1,0:T(4,128)S(1)} collective-permute-done((f32[1,128,4,2,128]{4,2,3,1,0:T(4,128)S(1)}, f32[1,128,4,2,128]{4,2,3,1,0:T(4,128)S(1)}, u32[]{:S(2)}, u32[]{:S(2)}) %collective-permute-start.3) | collective-permute-done | bytes 524320 | tf_op jit(solution)/shard_map/ppermute | solution.py:35
  115.8 10.1 %collective-permute-done.4 = f32[1,128,4,2,128]{4,2,3,1,0:T(4,128)S(1)} collective-permute-done((f32[1,128,4,2,128]{4,2,3,1,0:T(4,128)S(1)}, f32[1,128,4,2,128]{4,2,3,1,0:T(4,128)S(1)}, u32[]{:S(2)}, u32[]{:S(2)}) %collective-permute-start.4) | collective-permute-done | bytes 524320 | tf_op jit(solution)/shard_map/ppermute | solution.py:30
  126.0 0.1 fusion.84
  126.2 0.1 select_select_fusion.2
  126.3 0.1 fusion.80
  126.5 0.1 maximum_bitcast_fusion.1
  126.6 31.0 %fusion.1 = bf16[1,1,128,2,128,128]{5,4,3,2,1,0:T(8,128)(2,1)} fusion(f32[4,128,4,2,128]{4,2,3,1,0:T(4,128)S(1)} %constant_dynamic-update-slice_fusion, s32[]{:T(128)} %bitcast.25, pred[]{:T(512)} %bitcast.24, pred[]{:T(512)} %bitcast.22, f32[1,128,1,4,2,128]{5,3,4,1,2,0:T(4,128)S(1)} %maximum_bitcast_fusion.1, f32[1,128,1,4,2,128]{5,3,4,1,2,0:T(4,128)S(1)} %fusion.84), kind=kOutput, calls=%fused_computation.3 | convolution fusion | flops 411566080 | bytes 9961478 | tf_op jit(solution)/shard_map/vmap(fpwqa,fwqb->fpab)/dot_general | solution.py:80
  (21 shorter events, 0.7 us)
Async XLA Ops:
  6.5 98.9 %copy-start = (s32[4,2]{0,1:T(2,128)S(1)}, s32[4,2]{0,1:T(2,128)}, u32[]{:S(2)}) copy-start(s32[4,2]{0,1:T(2,128)} %param.7) | copy-start | bytes 100
  6.5 18.0 %all-gather.2.cloned.1.call-start = ((), (), s32[]{:S(2)}) async-start(), calls=%async_computation.1 | async-start | bytes 5529600 | tf_op jit(solution)/shard_map/all_gather | solution.py:87
  24.6 25.0 %copy-start.1 = (f32[128,2,3600]{0,2,1:T(8,128)S(1)}, f32[128,2,3600]{0,2,1:T(8,128)}, u32[]{:S(2)}) copy-start(f32[128,2,3600]{0,2,1:T(8,128)} %all-gather.2.cloned.1.call-done) | copy-start | bytes 11059204
  71.1 3.5 %collective-permute-start = (f32[10,2,128]{2,0,1:T(8,128)S(1)}, f32[10,2,128]{2,0,1:T(8,128)S(1)}, u32[]{:S(2)}, u32[]{:S(2)}) collective-permute-start(f32[10,2,128]{2,0,1:T(8,128)S(1)} %get-tuple-element.19), channel_id=1, source_target_pairs={{0,1},{2,3},{4,5},{6,7},{8,9},{10,11},{12,13},{14,15},{16,17},{18,... | collective-permute-start | bytes 30728 | tf_op jit(solution)/shard_map/ppermute | solution.py:52
  73.2 3.1 %collective-permute-start.1 = (f32[10,2,128]{2,0,1:T(8,128)S(1)}, f32[10,2,128]{2,0,1:T(8,128)S(1)}, u32[]{:S(2)}, u32[]{:S(2)}) collective-permute-start(f32[10,2,128]{2,0,1:T(8,128)S(1)} %get-tuple-element.20), channel_id=1, source_target_pairs={{1,0},{3,2},{5,4},{7,6},{9,8},{11,10},{13,12},{15,14},{17,16},{19,... | collective-permute-start | bytes 30728 | tf_op jit(solution)/shard_map/ppermute | solution.py:53
  88.6 16.8 %collective-permute-start.2 = (f32[1,128,4,2,128]{4,2,3,1,0:T(4,128)S(1)}, f32[1,128,4,2,128]{4,2,3,1,0:T(4,128)S(1)}, u32[]{:S(2)}, u32[]{:S(2)}) collective-permute-start(f32[1,128,4,2,128]{4,2,3,1,0:T(4,128)S(1)} %bitcast.66), channel_id=1, source_target_pairs={{0,4},{4,8},{8,12},{12,0},{1,5},{5,9},{9,13},{13,1},{2,6},{6,10},{... | collective-permute-start | bytes 1572872 | tf_op jit(solution)/shard_map/ppermute | solution.py:30
  90.3 25.4 %collective-permute-start.3 = (f32[1,128,4,2,128]{4,2,3,1,0:T(4,128)S(1)}, f32[1,128,4,2,128]{4,2,3,1,0:T(4,128)S(1)}, u32[]{:S(2)}, u32[]{:S(2)}) collective-permute-start(f32[1,128,4,2,128]{4,2,3,1,0:T(4,128)S(1)} %bitcast.67), channel_id=1, source_target_pairs={{0,12},{4,0},{8,4},{12,8},{1,13},{5,1},{9,5},{13,9},{2,14},{6,2},{... | collective-permute-start | bytes 1572872 | tf_op jit(solution)/shard_map/ppermute | solution.py:35
  105.4 20.6 %collective-permute-start.4 = (f32[1,128,4,2,128]{4,2,3,1,0:T(4,128)S(1)}, f32[1,128,4,2,128]{4,2,3,1,0:T(4,128)S(1)}, u32[]{:S(2)}, u32[]{:S(2)}) collective-permute-start(f32[1,128,4,2,128]{4,2,3,1,0:T(4,128)S(1)} %collective-permute-done.2), channel_id=1, source_target_pairs={{0,4},{4,8},{8,12},{12,0},{1,5},{5,9},{9,13},{13,1},{2,6},{6,10},{... | collective-permute-start | bytes 1572872 | tf_op jit(solution)/shard_map/ppermute | solution.py:30
Sparse Core Ops, SparseCore 0:
  8.9 15.6 all-gather.1
